TPU v7x, 512 devices: a whole 4x8x8 slice. The times are simulated.
512 devices in a mesh: feat: 32 (over x, z), tok: 16 (over y, core).
Axes of the slice: x: 4, y: 8, z: 8, core: 2. Of those that a mesh axis runs over, the one named last changes fastest.
Arguments:
- activations: bfloat16 [2048, 8192], P('tok', 'feat'), may hold values from -6 to 6
- w_base: bfloat16 [8192, 8192], P('feat', 'tok'), may hold values from -0.0625 to 0.0625
- blk_vals: bfloat16 [96, 128, 128], P('feat'), may hold values from -0.5 to 0.5
- blk_index: int32 [96, 2], P('feat'), may hold values from 0 to 63, as said below
- blk_count: int32 [32], P('feat'), may hold values from 1 to 3, as said below
- a_down: bfloat16 [8192, 64], P('feat'), may hold values from -0.0625 to 0.0625
- b_up: bfloat16 [64, 8192], P(None, 'feat'), may hold values from -0.75 to 0.75
- grad_out: bfloat16 [2048, 8192], P('tok', 'feat'), may hold values from -6 to 6
Outputs:
- projected: bfloat16 [2048, 8192], P('tok', 'feat')
- grad_x: bfloat16 [2048, 8192], P('tok', 'feat')
- grad_blocks: float32 [96, 128, 128], P('feat')
- grad_a: float32 [8192, 64], P('feat')
- grad_b: float32 [64, 8192], P(None, 'feat')
Inputs may be any that keep to these rules, and one draw needn't show every extreme that they name: `blk_index`: column 0 is below 2 and column 1 below 64; both largest values occur in every draw. `blk_count`: some feature shard holds exactly 3 live slots in every draw.
All inputs are finite; a program needn't handle non-finite values.
Results may differ from a plain program's by a relative error of at most 0.014.
Values may be sent and summed in bfloat16 or wider, within the bound.
A program may use at most 64 MiB of HBM per device.

v0:
```python
import jax
import jax.numpy as jnp
from jax import lax
from jax.sharding import PartitionSpec as P

BLK = 128


def on_device(activations, w_base, blk_vals, blk_index, blk_count, a_down, b_up, grad_out):
    tok_rows = activations.shape[0]
    grad_scale = float(tok_rows * lax.axis_size("tok")) ** (-0.5)
    live_count = blk_count[0]
    u_part = jnp.dot(activations, a_down, preferred_element_type=jnp.float32)
    v_part = jnp.dot(grad_out, b_up.T, preferred_element_type=jnp.float32)
    u_total = lax.psum(u_part, "feat")
    u_half = u_total.astype(jnp.bfloat16)
    w_rows = lax.all_gather(w_base, "tok", axis=1, tiled=True)
    partial_value = jnp.dot(activations, w_rows, preferred_element_type=jnp.float32)
    for slot_idx in range(blk_vals.shape[0]):
        is_live = (slot_idx < live_count).astype(jnp.float32)
        row_start = blk_index[slot_idx, 0] * BLK
        col_start = blk_index[slot_idx, 1] * BLK
        x_cols = lax.dynamic_slice_in_dim(activations, row_start, BLK, 1)
        forward_add = (
            jnp.dot(x_cols, blk_vals[slot_idx], preferred_element_type=jnp.float32) * is_live
        )
        current = lax.dynamic_slice_in_dim(partial_value, col_start, BLK, 1)
        partial_value = lax.dynamic_update_slice_in_dim(
            partial_value, current + forward_add, col_start, 1
        )
    own_sums = lax.psum_scatter(
        partial_value.astype(jnp.bfloat16), "feat", scatter_dimension=1, tiled=True
    ).astype(jnp.float32)
    projected = (own_sums + jnp.dot(u_half, b_up, preferred_element_type=jnp.float32)).astype(
        jnp.bfloat16
    )
    v_total = lax.psum(v_part, "feat")
    v_half = v_total.astype(jnp.bfloat16)
    cot_rows = lax.all_gather(grad_out, "feat", axis=1, tiled=True)
    backward = jnp.dot(cot_rows, w_rows.T, preferred_element_type=jnp.float32)
    block_terms = []
    for slot_idx in range(blk_vals.shape[0]):
        is_live = (slot_idx < live_count).astype(jnp.float32)
        row_start = blk_index[slot_idx, 0] * BLK
        col_start = blk_index[slot_idx, 1] * BLK
        x_cols = lax.dynamic_slice_in_dim(activations, row_start, BLK, 1)
        g_cols = lax.dynamic_slice_in_dim(cot_rows, col_start, BLK, 1)
        back_add = (
            jnp.dot(g_cols, blk_vals[slot_idx].T, preferred_element_type=jnp.float32) * is_live
        )
        current = lax.dynamic_slice_in_dim(backward, row_start, BLK, 1)
        backward = lax.dynamic_update_slice_in_dim(backward, current + back_add, row_start, 1)
        block_terms.append(jnp.dot(x_cols.T, g_cols, preferred_element_type=jnp.float32) * is_live)
    grad_x = (backward + jnp.dot(v_half, a_down.T, preferred_element_type=jnp.float32)).astype(
        jnp.bfloat16
    )
    block_local = jnp.stack(block_terms, axis=0)
    down_local = jnp.dot(activations.T, v_half, preferred_element_type=jnp.float32)
    up_local = jnp.dot(u_half.T, grad_out, preferred_element_type=jnp.float32)
    block_sum, down_sum, up_sum = lax.psum((block_local, down_local, up_local), "tok")
    return (projected, grad_x, block_sum * grad_scale, down_sum * grad_scale, up_sum * grad_scale)


def solution(mesh):
    in_specs = (
        P("tok", "feat"),
        P("feat", "tok"),
        P("feat", None, None),
        P("feat", None),
        P("feat"),
        P("feat", None),
        P(None, "feat"),
        P("tok", "feat"),
    )
    out_specs = (
        P("tok", "feat"),
        P("tok", "feat"),
        P("feat", None, None),
        P("feat", None),
        P(None, "feat"),
    )
    return jax.shard_map(
        on_device, mesh=mesh, in_specs=in_specs, out_specs=out_specs, check_vma=False
    )
```

profile of v0, /device:TPU:8, one launch (start us, length us, event | category | flops | bytes accessed | tf_op | source)
XLA Modules:
  0.0 517.7 jit_solution(15335018569101038187)
XLA Ops:
  7.2 0.7 all-gather.5.cloned.1.call-update
  8.0 0.7 all-gather.3.cloned.1.call-update
  8.7 1.6 fusion.55
  14.9 1.0 fusion.59
  15.9 0.9 fusion.57
  16.8 149.2 %all-reduce = (bf16[128,64]{0,1:T(8,128)(2,1)S(1)}, bf16[128,64]{0,1:T(8,128)(2,1)S(1)}) all-reduce(f32[128,64]{0,1:T(8,128)S(1)} %fusion.57, f32[128,64]{0,1:T(8,128)S(1)} %fusion.59), channel_id=1, replica_groups=mesh['feat'=32,'tok'=16] {'feat'}, use_global_device_ids=true, to_apply=%region_1.0 | all-reduce | flops 16384 | bytes 98304 | tf_op jit(solution)/shard_map/psum | solution.py:15
  165.9 1.6 fusion.60
  167.6 0.8 convolution_bitcast_fusion
  168.3 0.9 fusion.2
  169.3 0.9 fusion.3
  170.2 0.9 fusion.4
  171.2 0.7 pad_maximum_fusion
  172.0 2.9 fusion.56
  175.3 1.6 convert_element_type.45
  177.0 101.2 %all-reduce.4.cloned.1.call-done = (f32[3,128,128]{2,1,0:T(8,128)}, f32[256,64]{0,1:T(8,128)}, f32[64,256]{1,0:T(8,128)}) async-done(((f32[3,128,128]{2,1,0:T(8,128)}, f32[256,64]{0,1:T(8,128)}, f32[64,256]{1,0:T(8,128)}), (f32[3,128,128]{2,1,0:T(8,128)}, f32[256,64]{0,1:T(8,128)}, f32[64,256]{1,0:T(8,128)})) %all-reduce.4.cloned.1.call-update) | async-done | bytes 327696 | tf_op jit(solution)/shard_map/psum | solution.py:60
  278.2 1.5 broadcast_multiply_fusion.2
  279.7 1.5 broadcast_multiply_fusion.1
  281.2 1.6 broadcast_multiply_fusion
  282.8 3.7 fusion.58
  286.6 0.2 fusion.8
  286.8 0.2 fusion.6
  287.0 0.8 fusion.1
  287.8 221.7 %reduce-scatter.2.cloned.1.call-done = bf16[128,256]{1,0:T(8,128)(2,1)} async-done(((bf16[128,8192]{1,0:T(8,128)(2,1)}), bf16[128,256]{1,0:T(8,128)(2,1)}) %reduce-scatter.2.cloned.1.call-update) | async-done | bytes 65552 | tf_op jit(solution)/shard_map/reduce_scatter | solution.py:31
  509.5 1.7 fusion
  (22 shorter events, 0.8 us)
Async XLA Ops:
  7.2 8.7 %copy-start = (bf16[128,256]{1,0:T(8,128)(2,1)S(1)}, bf16[128,256]{1,0:T(8,128)(2,1)}, u32[]{:S(2)}) copy-start(bf16[128,256]{1,0:T(8,128)(2,1)} %param.8) | copy-start | bytes 196612
  7.2 161.1 %all-gather.5.cloned.1.call-start = ((), (), s32[]{:S(2)}) async-start(), calls=%async_computation.3 | async-start | bytes 2162688 | tf_op jit(solution)/shard_map/all_gather | solution.py:39
  7.9 164.1 %all-gather.3.cloned.1.call-start = ((), (), s32[]{:S(2)}) async-start(), calls=%async_computation.1 | async-start | bytes 4456448 | tf_op jit(solution)/shard_map/all_gather | solution.py:17
  8.7 269.5 %all-reduce.4.cloned.1.call-start = ((), (), s32[]{:S(2)}) async-start(), calls=%async_computation.4 | async-start | bytes 655360 | tf_op jit(solution)/shard_map/psum | solution.py:60
  171.9 3.0 copy-start.2
  171.9 337.6 %reduce-scatter.2.cloned.1.call-start = ((), (), s32[]{:S(2)}) async-start(), calls=%async_computation.2 | async-start | bytes 2162688 | tf_op jit(solution)/shard_map/reduce_scatter | solution.py:31
  175.3 107.4 %copy-start.1 = (bf16[128,8192]{1,0:T(8,128)(2,1)S(1)}, bf16[128,8192]{1,0:T(8,128)(2,1)}, u32[]{:S(2)}) copy-start(bf16[128,8192]{1,0:T(8,128)(2,1)} %all-gather.5.cloned.1.call-done) | copy-start | bytes 6291460
  177.0 110.0 %copy-start.3 = (bf16[256,64]{0,1:T(8,128)(2,1)S(1)}, bf16[256,64]{0,1:T(8,128)(2,1)}, u32[]{:S(2)}) copy-start(bf16[256,64]{0,1:T(8,128)(2,1)} %param.13) | copy-start | bytes 98308
  177.0 332.5 %copy-start.4 = (bf16[64,256]{1,0:T(8,128)(2,1)S(1)}, bf16[64,256]{1,0:T(8,128)(2,1)}, u32[]{:S(2)}) copy-start(bf16[64,256]{1,0:T(8,128)(2,1)} %param.14) | copy-start | bytes 98308
Sparse Core Ops, SparseCore 0:
  11.0 85.3 all-gather.4
  98.6 43.1 all-gather.2
  172.0 106.1 all-reduce.3
  282.5 226.9 reduce-scatter.1
where the time goes:
time: 518 us
  waiting for transfers between devices  324 us (63%)
  blocking collectives  149 us (29%)
  between operations  18.5 us (4%)
  matrix products  17.1 us (3%)
  other arithmetic  6.85 us (1%)
    reduce_scatter x1, waiting for transfers between devices, on_device(): lax.psum_scatter(partial_value.astype(jnp.bfloat16), 'feat', scatter_dime...  222 us
    psum x1, blocking collectives, on_device(): u_total = lax.psum(u_part, 'feat')  149 us
    psum x1, waiting for transfers between devices, on_device(): lax.psum((block_local, down_local, up_local), 'tok')  101 us
  transfers between devices with their start and end apart: 4, of which 2 were waited for; matrix products, arithmetic and copies ran while one was open for 5% of the time, Pallas kernels for 0%

commit v1 on v0

--- a/solution.py
+++ b/solution.py
@@ -6,13 +6,22 @@
 BLK = 128
 
 
+def sum_by_hops(array, name):
+    n_dev = lax.axis_size(name)
+    total, far = (array, 1)
+    while far < n_dev:
+        total = total + lax.ppermute(total, name, [(i, i ^ far) for i in range(n_dev)])
+        far = 2 * far
+    return total
+
+
 def on_device(activations, w_base, blk_vals, blk_index, blk_count, a_down, b_up, grad_out):
     tok_rows = activations.shape[0]
     grad_scale = float(tok_rows * lax.axis_size("tok")) ** (-0.5)
     live_count = blk_count[0]
     u_part = jnp.dot(activations, a_down, preferred_element_type=jnp.float32)
     v_part = jnp.dot(grad_out, b_up.T, preferred_element_type=jnp.float32)
-    u_total = lax.psum(u_part, "feat")
+    u_total = sum_by_hops(u_part, "feat")
     u_half = u_total.astype(jnp.bfloat16)
     w_rows = lax.all_gather(w_base, "tok", axis=1, tiled=True)
     partial_value = jnp.dot(activations, w_rows, preferred_element_type=jnp.float32)

time: 518 us -> 543 us (1.048)
  starting transfers between devices: 0.16 us -> 23.6 us
  waiting for transfers between devices: 324 us -> 334 us
  blocking collectives: 149 us -> 140 us
    ppermute x0 -> x5, starting transfers between devices: none -> 23.5 us  [sum_by_hops(): lax.ppermute(total, name, [(i, i ^ far) for i in range(n_dev)])]
    psum x1, blocking collectives: 149 us -> 140 us  [on_device(): v_total = lax.psum(v_part, 'feat')]
    ppermute x0 -> x5, waiting for transfers between devices: none -> 6.87 us  [sum_by_hops(): lax.ppermute(total, name, [(i, i ^ far) for i in range(n_dev)])]
  transfers between devices with their start and end apart: 4 -> 9, of which waited for: 2 -> 5; matrix products, arithmetic and copies ran while one was open for 5% -> 4% of each run, Pallas kernels for 0% -> 0%
where the time goes in v1:
time: 543 us; the launch traced here: 542 us
  waiting for transfers between devices  334 us (62%)
  blocking collectives  140 us (26%)
  starting transfers between devices  23.6 us (4%)
  between operations  18.4 us (3%)
  matrix products  17.1 us (3%)
  other arithmetic  6.9 us (1%)
    reduce_scatter x1, waiting for transfers between devices, on_device(): lax.psum_scatter(partial_value.astype(jnp.bfloat16), 'feat', scatter_dime...  222 us
    psum x1, blocking collectives, on_device(): v_total = lax.psum(v_part, 'feat')  140 us
    psum x1, waiting for transfers between devices, on_device(): lax.psum((block_local, down_local, up_local), 'tok')  105 us
    ppermute x5, starting transfers between devices, sum_by_hops(): lax.ppermute(total, name, [(i, i ^ far) for i in range(n_dev)])  23.5 us
  transfers between devices with their start and end apart: 9, of which 5 were waited for; matrix products, arithmetic and copies ran while one was open for 4% of the time, Pallas kernels for 0%

profile of v1, /device:TPU:8, one launch (start us, length us, event | category | flops | bytes accessed | tf_op | source)
XLA Modules:
  0.0 542.4 jit_solution(10395596056023935797)
XLA Ops:
  9.6 4.3 collective-permute-start
  13.9 1.9 collective-permute-done
  15.8 6.1 %collective-permute-start.1 = (f32[128,64]{0,1:T(8,128)S(1)}, f32[128,64]{0,1:T(8,128)S(1)}, u32[]{:S(2)}, u32[]{:S(2)}) collective-permute-start(f32[128,64]{0,1:T(8,128)S(1)} %add.91), channel_id=1, source_target_pairs={{0,32},{16,48},{32,0},{48,16},{64,96},{80,112},{96,64},{112,80},{1... | collective-permute-start | bytes 98312 | tf_op jit(solution)/shard_map/ppermute | solution.py:13
  21.9 1.9 collective-permute-done.1
  23.8 9.3 %collective-permute-start.2 = (f32[128,64]{0,1:T(8,128)S(1)}, f32[128,64]{0,1:T(8,128)S(1)}, u32[]{:S(2)}, u32[]{:S(2)}) collective-permute-start(f32[128,64]{0,1:T(8,128)S(1)} %add.92), channel_id=1, source_target_pairs={{0,64},{16,80},{32,96},{48,112},{64,0},{80,16},{96,32},{112,48},{1... | collective-permute-start | bytes 98312 | tf_op jit(solution)/shard_map/ppermute | solution.py:13
  33.1 1.0 fusion.56
  34.0 140.3 %psum.28 = bf16[128,64]{0,1:T(8,128)(2,1)S(1)} all-reduce(f32[128,64]{0,1:T(8,128)S(1)} %fusion.56), channel_id=1, replica_groups=mesh['feat'=32,'tok'=16] {'feat'}, use_global_device_ids=true, to_apply=%region_1.0 | all-reduce | flops 8192 | bytes 49152 | tf_op jit(solution)/shard_map/psum | solution.py:46
  174.4 1.9 collective-permute-start.3
  177.1 3.1 collective-permute-done.3
  180.2 1.9 collective-permute-start.4
  182.1 1.5 fusion.52
  188.1 1.6 fusion.57
  189.7 0.9 fusion.2
  190.7 0.9 fusion.3
  191.6 0.9 fusion.4
  193.4 2.9 fusion.53
  196.8 1.6 convert_element_type.45
  198.4 104.5 %all-reduce.3.cloned.1.call-done = (f32[3,128,128]{2,1,0:T(8,128)}, f32[256,64]{0,1:T(8,128)}, f32[64,256]{1,0:T(8,128)}) async-done(((f32[3,128,128]{2,1,0:T(8,128)}, f32[256,64]{0,1:T(8,128)}, f32[64,256]{1,0:T(8,128)}), (f32[3,128,128]{2,1,0:T(8,128)}, f32[256,64]{0,1:T(8,128)}, f32[64,256]{1,0:T(8,128)})) %all-reduce.3.cloned.1.call-update) | async-done | bytes 327696 | tf_op jit(solution)/shard_map/psum | solution.py:69
  302.9 1.5 broadcast_multiply_fusion.2
  304.4 1.5 broadcast_multiply_fusion.1
  305.9 1.6 broadcast_multiply_fusion
  307.5 3.7 fusion.55
  312.5 221.7 %reduce-scatter.2.cloned.1.call-done = bf16[128,256]{1,0:T(8,128)(2,1)} async-done(((bf16[128,8192]{1,0:T(8,128)(2,1)}), bf16[128,256]{1,0:T(8,128)(2,1)}) %reduce-scatter.2.cloned.1.call-update) | async-done | bytes 65552 | tf_op jit(solution)/shard_map/reduce_scatter | solution.py:40
  534.2 1.7 fusion
  (37 shorter events, 5.7 us)
Async XLA Ops:
  7.2 1.5 copy-start
  7.2 182.6 %all-gather.5.cloned.1.call-start = ((), (), s32[]{:S(2)}) async-start(), calls=%async_computation.3 | async-start | bytes 2162688 | tf_op jit(solution)/shard_map/all_gather | solution.py:48
  7.9 185.5 %all-gather.3.cloned.1.call-start = ((), (), s32[]{:S(2)}) async-start(), calls=%async_computation.1 | async-start | bytes 4456448 | tf_op jit(solution)/shard_map/all_gather | solution.py:26
  8.7 294.3 %all-reduce.3.cloned.1.call-start = ((), (), s32[]{:S(2)}) async-start(), calls=%async_computation.4 | async-start | bytes 655360 | tf_op jit(solution)/shard_map/psum | solution.py:69
  9.6 6.2 %collective-permute-start = (f32[128,64]{0,1:T(8,128)S(1)}, f32[128,64]{0,1:T(8,128)S(1)}, u32[]{:S(2)}, u32[]{:S(2)}) collective-permute-start(f32[128,64]{0,1:T(8,128)S(1)} %fusion.54), channel_id=1, source_target_pairs={{0,16},{16,0},{32,48},{48,32},{64,80},{80,64},{96,112},{112,96},{1... | collective-permute-start | bytes 98312 | tf_op jit(solution)/shard_map/ppermute | solution.py:13
  15.8 8.0 %collective-permute-start.1 = (f32[128,64]{0,1:T(8,128)S(1)}, f32[128,64]{0,1:T(8,128)S(1)}, u32[]{:S(2)}, u32[]{:S(2)}) collective-permute-start(f32[128,64]{0,1:T(8,128)S(1)} %add.91), channel_id=1, source_target_pairs={{0,32},{16,48},{32,0},{48,16},{64,96},{80,112},{96,64},{112,80},{1... | collective-permute-start | bytes 98312 | tf_op jit(solution)/shard_map/ppermute | solution.py:13
  23.8 150.6 %collective-permute-start.2 = (f32[128,64]{0,1:T(8,128)S(1)}, f32[128,64]{0,1:T(8,128)S(1)}, u32[]{:S(2)}, u32[]{:S(2)}) collective-permute-start(f32[128,64]{0,1:T(8,128)S(1)} %add.92), channel_id=1, source_target_pairs={{0,64},{16,80},{32,96},{48,112},{64,0},{80,16},{96,32},{112,48},{1... | collective-permute-start | bytes 98312 | tf_op jit(solution)/shard_map/ppermute | solution.py:13
  174.4 5.8 %collective-permute-start.3 = (f32[128,64]{0,1:T(8,128)S(1)}, f32[128,64]{0,1:T(8,128)S(1)}, u32[]{:S(2)}, u32[]{:S(2)}) collective-permute-start(f32[128,64]{0,1:T(8,128)S(1)} %add.93), channel_id=1, source_target_pairs={{0,128},{16,144},{32,160},{48,176},{64,192},{80,208},{96,224},{112... | collective-permute-start | bytes 98312 | tf_op jit(solution)/shard_map/ppermute | solution.py:13
  180.2 7.9 %collective-permute-start.4 = (f32[128,64]{0,1:T(8,128)S(1)}, f32[128,64]{0,1:T(8,128)S(1)}, u32[]{:S(2)}, u32[]{:S(2)}) collective-permute-start(f32[128,64]{0,1:T(8,128)S(1)} %add.94), channel_id=1, source_target_pairs={{0,256},{16,272},{32,288},{48,304},{64,320},{80,336},{96,352},{112... | collective-permute-start | bytes 98312 | tf_op jit(solution)/shard_map/ppermute | solution.py:13
  193.3 3.0 copy-start.2
  193.3 340.9 %reduce-scatter.2.cloned.1.call-start = ((), (), s32[]{:S(2)}) async-start(), calls=%async_computation.2 | async-start | bytes 2162688 | tf_op jit(solution)/shard_map/reduce_scatter | solution.py:40
  196.7 110.8 %copy-start.1 = (bf16[128,8192]{1,0:T(8,128)(2,1)S(1)}, bf16[128,8192]{1,0:T(8,128)(2,1)}, u32[]{:S(2)}) copy-start(bf16[128,8192]{1,0:T(8,128)(2,1)} %all-gather.5.cloned.1.call-done) | copy-start | bytes 6291460
  198.4 113.3 %copy-start.3 = (bf16[256,64]{0,1:T(8,128)(2,1)S(1)}, bf16[256,64]{0,1:T(8,128)(2,1)}, u32[]{:S(2)}) copy-start(bf16[256,64]{0,1:T(8,128)(2,1)} %param.13) | copy-start | bytes 98308
  198.4 335.8 %copy-start.4 = (bf16[64,256]{1,0:T(8,128)(2,1)S(1)}, bf16[64,256]{1,0:T(8,128)(2,1)}, u32[]{:S(2)}) copy-start(bf16[64,256]{1,0:T(8,128)(2,1)} %param.14) | copy-start | bytes 98308
Sparse Core Ops, SparseCore 0:
  11.0 85.4 all-gather.4
  98.6 43.2 all-gather.2
  193.4 109.4 all-reduce.2
  307.2 226.9 reduce-scatter.1
